TPU v7x, 32 devices: a whole 2x2x4 slice. The times are simulated.
32 devices in a mesh: dp: 8 (over z, y), expert: 4 (over x, core).
Axes of the slice: x: 2, y: 2, z: 4, core: 2. Of those that a mesh axis runs over, the one named last changes fastest.
Arguments:
- tokens: bfloat16 [4096, 2048], P(('dp', 'expert')), may hold values from -6 to 6
- routes: int32 [4096, 8], P(('dp', 'expert')), may hold values from 0 to 15, all different within a row; in each aligned block of 128 rows (0 to 127, 128 to 255, ...) at most 80 rows name the same one
- gates: bfloat16 [4096, 8], P(('dp', 'expert')), may hold values from 0.099609375 to 0.5
- cotangent: bfloat16 [4096, 2048], P(('dp', 'expert')), may hold values from -6 to 6
- w_gate: bfloat16 [16, 2048, 384], P('dp'), may hold values from -0.125 to 0.125
- w_up: bfloat16 [16, 2048, 384], P('dp'), may hold values from -0.125 to 0.125
- w_down: bfloat16 [16, 384, 2048], P('dp'), may hold values from -0.3125 to 0.3125
Outputs:
- layer_out: bfloat16 [4096, 2048], P(('dp', 'expert'))
- grad_tokens: bfloat16 [4096, 2048], P(('dp', 'expert'))
- grad_gate: bfloat16 [16, 2048, 384], P('dp', 'expert')
- grad_up: bfloat16 [16, 2048, 384], P('dp', 'expert')
- grad_down: bfloat16 [16, 384, 2048], P('dp', None, 'expert')
Inputs may be any that keep to these rules, and one draw needn't show every extreme that they name: `routes`: each row names 8 different experts. Among the rows of one device, no expert is named by more than 80 rows, and in every draw some device has an expert named by exactly 80 rows.
All inputs are finite; a program needn't handle non-finite values.
Results may differ from a plain program's by a relative error of at most 0.012.
Values may be sent and summed in bfloat16 or wider, within the bound.
A program may use at most 128 MiB of HBM per device.

v0:
```python
import jax
import jax.numpy as jnp
from jax import lax
from jax.sharding import PartitionSpec as P


def expert_forward(arrived, w_gate, w_up, w_down):
    gate_act = jnp.einsum("erd,edf->erf", arrived, w_gate, preferred_element_type=jnp.float32)
    up_act = jnp.einsum("erd,edf->erf", arrived, w_up, preferred_element_type=jnp.float32)
    sigma_gate = jax.nn.sigmoid(gate_act)
    smooth = gate_act * sigma_gate
    hidden = (smooth * up_act).astype(jnp.bfloat16)
    result = jnp.einsum("erf,efd->erd", hidden, w_down, preferred_element_type=jnp.float32).astype(
        jnp.bfloat16
    )
    return (gate_act, up_act, sigma_gate, smooth, hidden, result)


def body(tokens, routes, gates, cotangent, w_gate, w_up, w_down):
    tok_rows, top_k = routes.shape
    width = tokens.shape[1]
    owners = lax.axis_size("dp")
    me = lax.axis_index("dp")
    per_owner = w_gate.shape[0]
    hidden_units = w_gate.shape[2]
    experts = owners * per_owner
    capacity = max(2, tok_rows * top_k * 5 // (4 * experts))
    rows_per_expert = owners * capacity
    both = jnp.concatenate([tokens, cotangent], axis=1)
    all_both = lax.all_gather(both, "dp", axis=0, tiled=True)
    all_routes = lax.all_gather(routes, "dp", axis=0, tiled=True)
    all_gates = lax.all_gather(gates, "dp", axis=0, tiled=True)
    all_x = all_both[:, :width]
    all_c = all_both[:, width:]
    mine = me * per_owner + jnp.arange(per_owner, dtype=jnp.int32)
    hit = all_routes[None, :, :] == mine[:, None, None]
    named = jnp.any(hit, axis=2).astype(jnp.int32)
    gain = jnp.sum(jnp.where(hit, all_gates[None, :, :].astype(jnp.float32), 0.0), axis=2)
    position = jnp.where(named > 0, jnp.cumsum(named, axis=1) - 1, -1)
    pick = position[:, None, :] == jnp.arange(rows_per_expert, dtype=jnp.int32)[None, :, None]
    pick_x = pick.astype(jnp.bfloat16)
    pick_g = jnp.where(pick, gain[:, None, :], 0.0).astype(jnp.bfloat16)
    arrived = jnp.einsum("ept,td->epd", pick_x, all_x, preferred_element_type=jnp.float32).astype(
        jnp.bfloat16
    )
    arrived_grad = jnp.einsum(
        "ept,td->epd", pick_g, all_c, preferred_element_type=jnp.float32
    ).astype(jnp.bfloat16)
    state = expert_forward(arrived, w_gate, w_up, w_down)
    gate_act, up_act, sigma_gate, smooth, hidden, result = state
    out_part = jnp.einsum("ept,epd->td", pick_g, result, preferred_element_type=jnp.float32).astype(
        jnp.bfloat16
    )
    layer_out = lax.psum_scatter(out_part, "dp", scatter_dimension=0, tiled=True)
    grad_hidden = jnp.einsum(
        "erd,efd->erf", arrived_grad, w_down, preferred_element_type=jnp.float32
    )
    grad_upact = (grad_hidden * smooth).astype(jnp.bfloat16)
    grad_gateact = (
        grad_hidden * up_act * sigma_gate * (1.0 + gate_act * (1.0 - sigma_gate))
    ).astype(jnp.bfloat16)
    row_grads = (
        jnp.einsum("erf,edf->erd", grad_gateact, w_gate, preferred_element_type=jnp.float32)
        + jnp.einsum("erf,edf->erd", grad_upact, w_up, preferred_element_type=jnp.float32)
    ).astype(jnp.bfloat16)
    grad_part = jnp.einsum(
        "ept,epd->td", pick_x, row_grads, preferred_element_type=jnp.float32
    ).astype(jnp.bfloat16)
    grad_tokens = lax.psum_scatter(grad_part, "dp", scatter_dimension=0, tiled=True)
    both_factors = jnp.concatenate([grad_gateact, grad_upact], axis=2)
    input_term = jnp.einsum(
        "erd,erf->def", arrived, both_factors, preferred_element_type=jnp.float32
    )
    down_term = jnp.einsum("erf,erd->def", hidden, arrived_grad, preferred_element_type=jnp.float32)
    totals = lax.psum_scatter(
        jnp.concatenate([input_term, down_term], axis=2).astype(jnp.bfloat16),
        "expert",
        scatter_dimension=0,
        tiled=True,
    ).astype(jnp.float32)
    grad_gate = jnp.transpose(totals[:, :, :hidden_units], (1, 0, 2)).astype(jnp.bfloat16)
    grad_up = jnp.transpose(totals[:, :, hidden_units : 2 * hidden_units], (1, 0, 2)).astype(
        jnp.bfloat16
    )
    grad_down = jnp.transpose(totals[:, :, 2 * hidden_units :], (1, 2, 0)).astype(jnp.bfloat16)
    return (layer_out, grad_tokens, grad_gate, grad_up, grad_down)


def solution(mesh):
    return jax.shard_map(
        body,
        mesh=mesh,
        in_specs=(
            P(("dp", "expert"), None),
            P(("dp", "expert"), None),
            P(("dp", "expert"), None),
            P(("dp", "expert"), None),
            P("dp", None, None),
            P("dp", None, None),
            P("dp", None, None),
        ),
        out_specs=(
            P(("dp", "expert"), None),
            P(("dp", "expert"), None),
            P("dp", "expert", None),
            P("dp", "expert", None),
            P("dp", None, "expert"),
        ),
        check_vma=False,
    )
```

profile of v0, /device:TPU:0, one launch (start us, length us, event | category | flops | bytes accessed | tf_op | source)
XLA Modules:
  0.0 451.6 jit_solution(4144293296469988950)
XLA Ops:
  7.2 0.0 copy-start
  7.2 0.0 all-gather.2.cloned.1.call-start
  7.2 2.5 pad_maximum_fusion.1
  9.7 0.0 all-gather.2.cloned.1.call-update
  9.7 0.0 reduce-scatter.8.cloned.1.call-start
  9.8 28.8 %all_gather.10 = bf16[1024,8]{0,1:T(8,128)(2,1)S(1)} all-gather(bf16[128,8]{0,1:T(8,128)(2,1)} %param.9), channel_id=1, replica_groups=mesh['dp'=8,'expert'=4] {'dp'}, dimensions={0}, use_global_device_ids=true | all-gather | bytes 18432 | tf_op jit(solution)/shard_map/all_gather | solution.py:32
  38.6 31.7 %all_gather.9 = s32[1024,8]{0,1:T(8,128)S(1)} all-gather(s32[128,8]{0,1:T(8,128)} %param.8), channel_id=1, replica_groups=mesh['dp'=8,'expert'=4] {'dp'}, dimensions={0}, use_global_device_ids=true | all-gather | bytes 36864 | tf_op jit(solution)/shard_map/all_gather | solution.py:31
  70.3 0.1 compare_reduce_fusion
  70.4 0.6 reduce-window.6
  71.0 0.2 slice_reduce_fusion
  71.2 0.2 reduce-window.9
  71.4 0.1 fusion.26
  71.5 0.1 add_bitcast_fusion
  71.6 66.1 %all-gather.2.cloned.1.call-done = bf16[1024,4096]{1,0:T(8,128)(2,1)} async-done(((bf16[128,4096]{1,0:T(8,128)(2,1)}), bf16[1024,4096]{1,0:T(8,128)(2,1)}) %all-gather.2.cloned.1.call-update) | async-done | bytes 8388624 | tf_op jit(solution)/shard_map/all_gather | solution.py:30
  137.7 0.0 copy-start.3
  137.7 8.4 %fusion.6 = bf16[2,640,2048]{2,1,0:T(8,128)(2,1)S(1)} fusion(bf16[1024,4096]{1,0:T(8,128)(2,1)} %all-gather.2.cloned.1.call-done, s32[2,1024]{1,0:T(2,128)S(1)} %compare_select_fusion.1), kind=kOutput, calls=%fused_computation.15 | convolution fusion | flops 5372641280 | bytes 9445376 | tf_op jit(solution)/shard_map/ept,td->epd/dot_general | solution.py:43
  146.1 0.0 copy-done.3
  146.1 0.0 copy-start.1
  146.1 0.0 slice-start
  146.2 2.9 fusion.31
  149.0 0.0 copy-done.1
  149.1 0.0 slice-start.1
  149.1 4.1 fusion.30
  153.2 0.0 slice-done
  153.2 0.0 slice-done.1
  153.2 7.9 %fusion.5 = bf16[2,640,2048]{2,1,0:T(8,128)(2,1)} fusion(bf16[1024,4096]{1,0:T(8,128)(2,1)S(1)} %bitcast.63, bf16[2,1024]{1,0:T(2,128)(2,1)S(1)} %fusion.26, s32[2,1024]{1,0:T(2,128)S(1)} %compare_select_fusion.1), kind=kOutput, calls=%fused_computation.14 | convolution fusion | flops 5373952000 | bytes 9449472 | tf_op jit(solution)/shard_map/ept,td->epd/dot_general | solution.py:46
  161.1 0.0 copy-done
  161.1 0.0 copy-start.5
  161.1 6.5 %multiply_convert_fusion = (bf16[2,640,384]{1,2,0:T(8,128)(2,1)S(1)}, bf16[2,640,384]{1,2,0:T(8,128)(2,1)S(1)}, bf16[2,640,384]{1,2,0:T(8,128)(2,1)S(1)}) fusion(f32[2,640,384]{1,2,0:T(8,128)} %fusion.30, f32[2,640,384]{1,2,0:T(8,128)S(1)} %fusion.31, bf16[2,640,2048]{2,1,0:T(8,128)(2,1)} %fusion.5, bf16[2,384,2048]{2,1,0:T(8,128)(2,1)S(1)} %copy-done), kind=kOutput, calls=%fused_computation.30 | convolution fusion | flops 2020638720 | bytes 15269888 | tf_op jit(solution)/shard_map/erd,efd->erf/dot_general | solution.py:55
  167.6 0.0 copy-start.4
  167.6 0.0 copy-start.2
  167.6 0.0 copy-start.6
  167.7 0.0 copy-done.5
  167.7 2.9 fusion.9
  170.5 0.0 copy-done.4
  170.5 0.0 copy-done.2
  170.6 0.0 copy-done.6
  170.6 5.3 %convert_bitcast_fusion = bf16[2048,2,768]{0,2,1:T(8,128)(2,1)S(1)} fusion(bf16[2,640,2048]{2,1,0:T(8,128)(2,1)S(1)} %fusion.6, bf16[2,640,384]{1,2,0:T(8,128)(2,1)S(1)} %get-tuple-element.20, bf16[2,640,384]{1,2,0:T(8,128)(2,1)S(1)} %get-tuple-element.21), kind=kOutput, calls=%fused_computation.4 | convolution fusion | flops 4033609728 | bytes 13500416 | tf_op jit(solution)/shard_map/erd,erf->def/dot_general | solution.py:71
  175.9 8.5 %pad_maximum_fusion = bf16[2048,2,1152]{0,2,1:T(8,128)(2,1)} fusion(bf16[2048,2,384]{0,2,1:T(8,128)(2,1)S(1)} %fusion.9, bf16[2048,2,768]{0,2,1:T(8,128)(2,1)S(1)} %convert_bitcast_fusion), kind=kLoop, calls=%fused_computation.1 | loop fusion | flops 18874368 | bytes 18874368 | tf_op jit(solution)/shard_map/concatenate | solution.py:76
  184.3 0.0 reduce-scatter.8.cloned.1.call-update
  184.4 0.0 reduce-scatter.4.cloned.1.call-start
  184.4 4.4 fusion.59
  188.8 7.4 %bitcast_convert_fusion.1 = bf16[1024,2048]{1,0:T(8,128)(2,1)} fusion(bf16[2,1024]{1,0:T(2,128)(2,1)S(1)} %fusion.26, s32[2,1024]{1,0:T(2,128)S(1)} %compare_select_fusion.1, bf16[2,640,2048]{2,1,0:T(8,128)(2,1)S(1)} %fusion.59), kind=kOutput, calls=%fused_computation.3 | convolution fusion | flops 5373427712 | bytes 9449472 | tf_op jit(solution)/shard_map/ept,epd->td/dot_general | solution.py:51
  196.2 0.0 reduce-scatter.4.cloned.1.call-update
  196.2 0.3 reduce-scatter.6.cloned.1.call-start
  196.5 9.6 %fusion.32 = f32[2,640,2048]{2,1,0:T(8,128)} fusion(bf16[2,640,384]{1,2,0:T(8,128)(2,1)} %copy-done.2, bf16[2,2048,384]{2,1,0:T(8,128)(2,1)} %param.11), kind=kOutput, calls=%fused_computation.54 | convolution fusion | flops 2013265920 | bytes 14614528 | tf_op jit(solution)/shard_map/erf,edf->erd/dot_general | solution.py:63
  206.1 16.5 %bitcast_convert_fusion = bf16[1024,2048]{1,0:T(8,128)(2,1)} fusion(f32[2,640,2048]{2,1,0:T(8,128)} %fusion.32, s32[2,1024]{1,0:T(2,128)S(1)} %compare_select_fusion.1, bf16[2,640,384]{1,2,0:T(8,128)(2,1)} %copy-done.6, bf16[2,2048,384]{2,1,0:T(8,128)(2,1)} %param.12), kind=kOutput, calls=%fused_computation.2 | convolution fusion | flops 7390625792 | bytes 18817024 | tf_op jit(solution)/shard_map/ept,epd->td/dot_general | solution.py:66
  222.6 0.0 reduce-scatter.6.cloned.1.call-update
  222.6 37.9 %reduce-scatter.8.cloned.1.call-done = bf16[512,2,1152]{0,2,1:T(8,128)(2,1)} async-done(((bf16[2048,2,1152]{0,2,1:T(8,128)(2,1)}), bf16[512,2,1152]{0,2,1:T(8,128)(2,1)}) %reduce-scatter.8.cloned.1.call-update) | async-done | bytes 2359312 | tf_op jit(solution)/shard_map/reduce_scatter | solution.py:75
  260.5 3.1 slice_bitcast_fusion.8
  263.6 2.3 copy.36
  265.8 2.3 copy.35
  268.1 84.9 %reduce-scatter.4.cloned.1.call-done = bf16[128,2048]{1,0:T(8,128)(2,1)} async-done(((bf16[1024,2048]{1,0:T(8,128)(2,1)}), bf16[128,2048]{1,0:T(8,128)(2,1)}) %reduce-scatter.4.cloned.1.call-update) | async-done | bytes 524304 | tf_op jit(solution)/shard_map/reduce_scatter | solution.py:54
  353.1 92.0 %reduce-scatter.6.cloned.1.call-done = bf16[128,2048]{1,0:T(8,128)(2,1)} async-done(((bf16[1024,2048]{1,0:T(8,128)(2,1)}), bf16[128,2048]{1,0:T(8,128)(2,1)}) %reduce-scatter.6.cloned.1.call-update) | async-done | bytes 524304 | tf_op jit(solution)/shard_map/reduce_scatter | solution.py:69
  (6 shorter events, 0.0 us)
Async XLA Ops:
  7.2 154.0 %copy-start = (bf16[2,384,2048]{2,1,0:T(8,128)(2,1)S(1)}, bf16[2,384,2048]{2,1,0:T(8,128)(2,1)}, u32[]{:S(2)}) copy-start(bf16[2,384,2048]{2,1,0:T(8,128)(2,1)} %param.13) | copy-start | bytes 9437188
  7.2 130.6 %all-gather.2.cloned.1.call-start = ((), (), s32[]{:S(2)}) async-start(), calls=%async_computation.3 | async-start | bytes 9437184 | tf_op jit(solution)/shard_map/all_gather | solution.py:30
  9.7 250.8 %reduce-scatter.8.cloned.1.call-start = ((), (), s32[]{:S(2)}) async-start(), calls=%async_computation.6 | async-start | bytes 11796480 | tf_op jit(solution)/shard_map/reduce_scatter | solution.py:75
  137.7 8.4 %copy-start.3 = (bf16[2,2048,384]{2,1,0:T(8,128)(2,1)S(1)}, bf16[2,2048,384]{2,1,0:T(8,128)(2,1)}, u32[]{:S(2)}) copy-start(bf16[2,2048,384]{2,1,0:T(8,128)(2,1)} %param.12) | copy-start | bytes 9437188
  146.1 2.9 copy-start.1
  146.1 7.1 %slice-start = ((s8[8388608]{0:T(1024)(128)(4,1)}), s8[4194304]{0:T(1024)(128)(4,1)S(1)}, s32[]{:S(2)}) async-start(s8[8388608]{0:T(1024)(128)(4,1)} %bitcast.62), calls=%async_computation.7 | async-start | bytes 8388608
  149.1 4.2 slice-start.1
  161.1 6.5 %copy-start.5 = (bf16[2,640,2048]{2,1,0:T(8,128)(2,1)S(1)}, bf16[2,640,2048]{2,1,0:T(8,128)(2,1)}, u32[]{:S(2)}) copy-start(bf16[2,640,2048]{2,1,0:T(8,128)(2,1)} %fusion.5) | copy-start | bytes 15728644
  167.6 2.9 copy-start.4
  167.6 2.9 copy-start.2
  167.6 2.9 copy-start.6
  184.4 168.7 %reduce-scatter.4.cloned.1.call-start = ((), (), s32[]{:S(2)}) async-start(), calls=%async_computation.4 | async-start | bytes 4718592 | tf_op jit(solution)/shard_map/reduce_scatter | solution.py:54
  196.2 248.8 %reduce-scatter.6.cloned.1.call-start = ((), (), s32[]{:S(2)}) async-start(), calls=%async_computation.5 | async-start | bytes 4718592 | tf_op jit(solution)/shard_map/reduce_scatter | solution.py:69
Sparse Core Ops, SparseCore 0:
  10.1 127.5 all-gather.1
  184.5 75.9 reduce-scatter.7
  264.7 88.2 reduce-scatter.3
  357.1 87.9 reduce-scatter.5
where the time goes:
time: 452 us
  waiting for transfers between devices  281 us (62%)
  matrix products  75.8 us (17%)
  blocking collectives  60.5 us (13%)
  between operations  14 us (3%)
  other arithmetic  12 us (3%)
  local copies, waits for them, and re-layouts  7.89 us (2%)
    reduce_scatter x1, waiting for transfers between devices, body(): lax.psum_scatter(grad_part, 'dp', scatter_dimension=0, tiled=True)  92 us
    reduce_scatter x1, waiting for transfers between devices, body(): lax.psum_scatter(out_part, 'dp', scatter_dimension=0, tiled=True)  84.9 us
    all_gather x1, waiting for transfers between devices, body(): all_both = lax.all_gather(both, 'dp', axis=0, tiled=True)  66.1 us
    reduce_scatter x1, waiting for transfers between devices, body(): lax.psum_scatter(jnp.concatenate([input_term, down_term], axis=2).astype(...  37.9 us
    all_gather x1, blocking collectives, body(): all_routes = lax.all_gather(routes, 'dp', axis=0, tiled=True)  31.7 us
    all_gather x1, blocking collectives, body(): all_gates = lax.all_gather(gates, 'dp', axis=0, tiled=True)  28.8 us
    dot_general x1, matrix products, body(): jnp.einsum('ept,epd->td', pick_x, row_grads, preferred_element_type=jnp.f...  16.5 us
    dot_general x1, matrix products, body(): jnp.einsum('erf,edf->erd', grad_gateact, w_gate, preferred_element_type=j...  9.57 us
  transfers between devices with their start and end apart: 4, of which 4 were waited for; matrix products, arithmetic and copies ran while one was open for 10% of the time, Pallas kernels for 0%

commit v1 on v0

--- a/solution.py
+++ b/solution.py
@@ -2,6 +2,24 @@
 import jax.numpy as jnp
 from jax import lax
 from jax.sharding import PartitionSpec as P
+
+
+def in_order(blocks, dim):
+    blocks = jnp.moveaxis(blocks, 0, dim)
+    dims = blocks.shape
+    return blocks.reshape(*dims[:dim], dims[dim] * dims[dim + 1], *dims[dim + 2 :])
+
+
+def doubled(array, axis):
+    length = lax.axis_size(axis)
+    blocks = array[None]
+    for level in range(length.bit_length() - 1):
+        stride = 1 << level
+        other = lax.ppermute(blocks, axis, [(i, i ^ stride) for i in range(length)])
+        both = jnp.stack([blocks, other])
+        upper = lax.axis_index(axis) >> level & 1
+        blocks = jnp.where(upper == 0, both, both[::-1]).reshape(-1, *array.shape)
+    return blocks
 
 
 def expert_forward(arrived, w_gate, w_up, w_down):
@@ -27,7 +45,7 @@
     capacity = max(2, tok_rows * top_k * 5 // (4 * experts))
     rows_per_expert = owners * capacity
     both = jnp.concatenate([tokens, cotangent], axis=1)
-    all_both = lax.all_gather(both, "dp", axis=0, tiled=True)
+    all_both = in_order(doubled(both, "dp"), 0)
     all_routes = lax.all_gather(routes, "dp", axis=0, tiled=True)
     all_gates = lax.all_gather(gates, "dp", axis=0, tiled=True)
     all_x = all_both[:, :width]

time: 452 us -> 674 us (1.49)
  blocking collectives: 60.5 us -> 231 us
  other arithmetic: 12 us -> 40.3 us
  matrix products: 75.8 us -> 83.7 us
  starting transfers between devices: 0.38 us -> 7.63 us
    all_gather x1, blocking collectives: 28.8 us -> 200 us  [body(): all_gates = lax.all_gather(gates, 'dp', axis=0, tiled=True)]
    ppermute x0 -> x3, waiting for transfers between devices: none -> 68.8 us  [doubled(): other = lax.ppermute(blocks, axis, [(i, i ^ stride) for i in range(length)])]
    all_gather x1 -> x0, waiting for transfers between devices: 66.1 us -> none  [body(): all_both = lax.all_gather(both, 'dp', axis=0, tiled=True)]
    select_n x0 -> x2, other arithmetic: none -> 16.4 us  [doubled(): blocks = jnp.where(upper == 0, both, both[::-1]).reshape(-1, *array.shape)]
    another operation x2 -> x6, other arithmetic: 0.77 us -> 15.1 us  [the longest x4 14.3 us: doubled(): both = jnp.stack([blocks, other])]
    dot_general x1, matrix products: 7.89 us -> 17.6 us  [body(): jnp.einsum('ept,td->epd', pick_g, all_c, preferred_element_type=jnp.float32)]
    ppermute x0 -> x3, starting transfers between devices: none -> 7.33 us  [doubled(): other = lax.ppermute(blocks, axis, [(i, i ^ stride) for i in range(length)])]
  transfers between devices with their start and end apart: 4 -> 6, of which waited for: 4 -> 5; matrix products, arithmetic and copies ran while one was open for 10% -> 7% of each run, Pallas kernels for 0% -> 0%
where the time goes in v1:
time: 674 us; the launch traced here: 671 us
  waiting for transfers between devices  283 us (42%)
  blocking collectives  231 us (34%)
  matrix products  83.7 us (12%)
  other arithmetic  40.3 us (6%)
  between operations  14.2 us (2%)
  local copies, waits for them, and re-layouts  11.9 us (2%)
  starting transfers between devices  7.63 us (1%)
    all_gather x1, blocking collectives, body(): all_gates = lax.all_gather(gates, 'dp', axis=0, tiled=True)  200 us
    reduce_scatter x1, waiting for transfers between devices, body(): lax.psum_scatter(grad_part, 'dp', scatter_dimension=0, tiled=True)  92.2 us
    reduce_scatter x1, waiting for transfers between devices, body(): lax.psum_scatter(out_part, 'dp', scatter_dimension=0, tiled=True)  84.9 us
    ppermute x3, waiting for transfers between devices, doubled(): other = lax.ppermute(blocks, axis, [(i, i ^ stride) for i in range(length)])  68.8 us
    reduce_scatter x1, waiting for transfers between devices, body(): lax.psum_scatter(jnp.concatenate([input_term, down_term], axis=2).astype(...  37.2 us
    all_gather x1, blocking collectives, body(): all_routes = lax.all_gather(routes, 'dp', axis=0, tiled=True)  31 us
    dot_general x1, matrix products, body(): jnp.einsum('ept,td->epd', pick_g, all_c, preferred_element_type=jnp.float32)  17.6 us
    select_n x2, other arithmetic, doubled(): blocks = jnp.where(upper == 0, both, both[::-1]).reshape(-1, *array.shape)  16.4 us
  transfers between devices with their start and end apart: 6, of which 5 were waited for; matrix products, arithmetic and copies ran while one was open for 7% of the time, Pallas kernels for 0%

profile of v1, /device:TPU:0, one launch (start us, length us, event | category | flops | bytes accessed | tf_op | source)
XLA Modules:
  0.0 671.5 jit_solution(12233276144147664108)
XLA Ops:
  7.2 0.0 copy-start
  7.2 0.0 reduce-scatter.8.cloned.1.call-start
  7.2 2.1 constant_dynamic-update-slice_fusion.1
  9.3 1.9 constant_dynamic-update-slice_fusion
  11.2 3.0 collective-permute-start
  14.2 23.5 %collective-permute-done = bf16[1,128,4096]{2,1,0:T(8,128)(2,1)} collective-permute-done((bf16[1,128,4096]{2,1,0:T(8,128)(2,1)}, bf16[1,128,4096]{2,1,0:T(8,128)(2,1)}, u32[]{:S(2)}, u32[]{:S(2)}) %collective-permute-start) | collective-permute-done | bytes 1048608 | tf_op jit(solution)/shard_map/ppermute | solution.py:18
  37.7 1.7 pad_maximum_fusion.3
  39.4 2.6 fusion.25
  42.0 1.8 collective-permute-start.1
  43.8 45.3 %collective-permute-done.1 = bf16[2,128,4096]{2,1,0:T(8,128)(2,1)} collective-permute-done((bf16[2,128,4096]{2,1,0:T(8,128)(2,1)}, bf16[2,128,4096]{2,1,0:T(8,128)(2,1)}, u32[]{:S(2)}, u32[]{:S(2)}) %collective-permute-start.1) | collective-permute-done | bytes 2097184 | tf_op jit(solution)/shard_map/ppermute | solution.py:18
  89.1 2.6 pad_maximum_fusion.2
  91.7 0.0 copy-start.5
  91.7 0.0 copy-start.4
  91.7 2.9 reverse_select_fusion.1
  94.6 2.5 collective-permute-start.2
  97.1 0.0 copy-done.5
  97.1 199.7 %all_gather.7 = bf16[1024,8]{0,1:T(8,128)(2,1)S(1)} all-gather(bf16[128,8]{0,1:T(8,128)(2,1)S(1)} %copy-done.5), channel_id=1, replica_groups=mesh['dp'=8,'expert'=4] {'dp'}, dimensions={0}, use_global_device_ids=true | all-gather | bytes 18432 | tf_op jit(solution)/shard_map/all_gather | solution.py:50
  296.9 0.0 copy-done.4
  296.9 31.0 %all_gather.6 = s32[1024,8]{0,1:T(8,128)S(1)} all-gather(s32[128,8]{0,1:T(8,128)S(1)} %copy-done.4), channel_id=1, replica_groups=mesh['dp'=8,'expert'=4] {'dp'}, dimensions={0}, use_global_device_ids=true | all-gather | bytes 36864 | tf_op jit(solution)/shard_map/all_gather | solution.py:49
  327.9 0.1 compare_reduce_fusion
  328.0 0.6 reduce-window.6
  328.6 0.2 slice_reduce_fusion
  328.8 0.2 reduce-window.9
  329.0 0.1 fusion.28
  329.1 0.1 add_bitcast_fusion
  329.2 0.0 collective-permute-done.2
  329.2 7.5 %pad_maximum_fusion.1 = bf16[2,4,128,4096]{3,2,1,0:T(8,128)(2,1)} fusion(bf16[1,4,128,4096]{3,2,1,0:T(8,128)(2,1)} %bitcast.8, bf16[1,4,128,4096]{3,2,1,0:T(8,128)(2,1)} %bitcast.6), kind=kLoop, calls=%fused_computation.3 | loop fusion | flops 4194304 | bytes 16777216 | tf_op jit(solution)/shard_map/stack | solution.py:19
  336.6 13.5 %reverse_select_fusion = bf16[2,4,128,4096]{3,2,1,0:T(8,128)(2,1)} fusion(bf16[2,4,128,4096]{3,2,1,0:T(8,128)(2,1)} %pad_maximum_fusion.1, pred[]{:T(512)S(6)} %eq.41), kind=kLoop, calls=%fused_computation | loop fusion | flops 4194304 | bytes 16777216 | tf_op jit(solution)/shard_map/jit(_where)/select_n | solution.py:21
  350.2 0.0 copy-start.1
  350.2 8.4 %fusion.6 = bf16[2,640,2048]{2,1,0:T(8,128)(2,1)S(1)} fusion(bf16[1024,4096]{1,0:T(8,128)(2,1)} %bitcast.72, s32[2,1024]{1,0:T(2,128)S(1)} %compare_select_fusion.1), kind=kOutput, calls=%fused_computation.19 | convolution fusion | flops 5372641280 | bytes 9445376 | tf_op jit(solution)/shard_map/ept,td->epd/dot_general | solution.py:61
  358.5 0.0 copy-done.1
  358.6 0.0 copy-start.6
  358.6 17.6 %fusion.5 = bf16[2,640,2048]{2,1,0:T(8,128)(2,1)S(1)} fusion(bf16[1024,4096]{1,0:T(8,128)(2,1)S(1)} %bitcast.73, bf16[2,1024]{1,0:T(2,128)(2,1)S(1)} %fusion.28, s32[2,1024]{1,0:T(2,128)S(1)} %compare_select_fusion.1), kind=kOutput, calls=%fused_computation.18 | convolution fusion | flops 5373952000 | bytes 9449472 | tf_op jit(solution)/shard_map/ept,td->epd/dot_general | solution.py:64
  376.2 0.0 copy-done.6
  376.2 0.0 copy-start.2
  376.2 2.9 fusion.33
  379.1 0.0 copy-done.2
  379.1 4.1 fusion.32
  383.2 0.0 copy-done
  383.2 4.9 multiply_convert_fusion
  388.1 0.0 copy-start.7
  388.1 0.0 copy-start.3
  388.2 0.0 copy-start.8
  388.2 2.9 fusion.9
  391.0 0.0 copy-done.7
  391.1 0.0 copy-done.3
  391.1 0.0 copy-done.8
  391.1 5.3 convert_bitcast_fusion
  396.4 8.5 %pad_maximum_fusion = bf16[2048,2,1152]{0,2,1:T(8,128)(2,1)} fusion(bf16[2048,2,384]{0,2,1:T(8,128)(2,1)S(1)} %fusion.9, bf16[2048,2,768]{0,2,1:T(8,128)(2,1)S(1)} %convert_bitcast_fusion), kind=kLoop, calls=%fused_computation.2 | loop fusion | flops 18874368 | bytes 18874368 | tf_op jit(solution)/shard_map/concatenate | solution.py:94
  404.8 0.0 reduce-scatter.8.cloned.1.call-update
  404.9 0.0 reduce-scatter.4.cloned.1.call-start
  404.9 4.4 fusion.61
  409.3 7.4 %bitcast_convert_fusion.1 = bf16[1024,2048]{1,0:T(8,128)(2,1)} fusion(bf16[2,1024]{1,0:T(2,128)(2,1)S(1)} %fusion.28, s32[2,1024]{1,0:T(2,128)S(1)} %compare_select_fusion.1, bf16[2,640,2048]{2,1,0:T(8,128)(2,1)S(1)} %fusion.61), kind=kOutput, calls=%fused_computation.5 | convolution fusion | flops 5373427712 | bytes 9449472 | tf_op jit(solution)/shard_map/ept,epd->td/dot_general | solution.py:69
  416.7 0.0 reduce-scatter.4.cloned.1.call-update
  416.7 0.2 reduce-scatter.6.cloned.1.call-start
  416.9 9.8 %fusion.34 = f32[2,640,2048]{2,1,0:T(8,128)} fusion(bf16[2,640,384]{1,2,0:T(8,128)(2,1)} %copy-done.3, bf16[2,2048,384]{2,1,0:T(8,128)(2,1)} %param.11), kind=kOutput, calls=%fused_computation.63 | convolution fusion | flops 2013265920 | bytes 14614528 | tf_op jit(solution)/shard_map/erf,edf->erd/dot_general | solution.py:81
  426.7 16.1 %bitcast_convert_fusion = bf16[1024,2048]{1,0:T(8,128)(2,1)} fusion(f32[2,640,2048]{2,1,0:T(8,128)} %fusion.34, s32[2,1024]{1,0:T(2,128)S(1)} %compare_select_fusion.1, bf16[2,640,384]{1,2,0:T(8,128)(2,1)} %copy-done.8, bf16[2,2048,384]{2,1,0:T(8,128)(2,1)} %param.12), kind=kOutput, calls=%fused_computation.4 | convolution fusion | flops 7390625792 | bytes 18817024 | tf_op jit(solution)/shard_map/ept,epd->td/dot_general | solution.py:84
  442.8 0.0 reduce-scatter.6.cloned.1.call-update
  442.8 37.2 %reduce-scatter.8.cloned.1.call-done = bf16[512,2,1152]{0,2,1:T(8,128)(2,1)} async-done(((bf16[2048,2,1152]{0,2,1:T(8,128)(2,1)}), bf16[512,2,1152]{0,2,1:T(8,128)(2,1)}) %reduce-scatter.8.cloned.1.call-update) | async-done | bytes 2359312 | tf_op jit(solution)/shard_map/reduce_scatter | solution.py:93
  480.0 3.1 slice_bitcast_fusion.8
  483.1 2.3 copy.36
  485.4 2.3 copy.35
  487.7 84.9 %reduce-scatter.4.cloned.1.call-done = bf16[128,2048]{1,0:T(8,128)(2,1)} async-done(((bf16[1024,2048]{1,0:T(8,128)(2,1)}), bf16[128,2048]{1,0:T(8,128)(2,1)}) %reduce-scatter.4.cloned.1.call-update) | async-done | bytes 524304 | tf_op jit(solution)/shard_map/reduce_scatter | solution.py:72
  572.6 92.2 %reduce-scatter.6.cloned.1.call-done = bf16[128,2048]{1,0:T(8,128)(2,1)} async-done(((bf16[1024,2048]{1,0:T(8,128)(2,1)}), bf16[128,2048]{1,0:T(8,128)(2,1)}) %reduce-scatter.6.cloned.1.call-update) | async-done | bytes 524304 | tf_op jit(solution)/shard_map/reduce_scatter | solution.py:87
  (5 shorter events, 0.0 us)
Async XLA Ops:
  7.2 376.0 %copy-start = (bf16[2,384,2048]{2,1,0:T(8,128)(2,1)S(1)}, bf16[2,384,2048]{2,1,0:T(8,128)(2,1)}, u32[]{:S(2)}) copy-start(bf16[2,384,2048]{2,1,0:T(8,128)(2,1)} %param.13) | copy-start | bytes 9437188
  7.2 472.8 %reduce-scatter.8.cloned.1.call-start = ((), (), s32[]{:S(2)}) async-start(), calls=%async_computation.5 | async-start | bytes 11796480 | tf_op jit(solution)/shard_map/reduce_scatter | solution.py:93
  11.2 26.5 %collective-permute-start = (bf16[1,128,4096]{2,1,0:T(8,128)(2,1)}, bf16[1,128,4096]{2,1,0:T(8,128)(2,1)}, u32[]{:S(2)}, u32[]{:S(2)}) collective-permute-start(bf16[1,128,4096]{2,1,0:T(8,128)(2,1)} %bitcast.1), channel_id=1, source_target_pairs={{0,4},{4,0},{8,12},{12,8},{16,20},{20,16},{24,28},{28,24},{1,5},{5... | collective-permute-start | bytes 3145736 | tf_op jit(solution)/shard_map/ppermute | solution.py:18
  42.0 47.1 %collective-permute-start.1 = (bf16[2,128,4096]{2,1,0:T(8,128)(2,1)}, bf16[2,128,4096]{2,1,0:T(8,128)(2,1)}, u32[]{:S(2)}, u32[]{:S(2)}) collective-permute-start(bf16[2,128,4096]{2,1,0:T(8,128)(2,1)} %get-tuple-element.27), channel_id=1, source_target_pairs={{0,8},{4,12},{8,0},{12,4},{16,24},{20,28},{24,16},{28,20},{1,9},{5... | collective-permute-start | bytes 6291464 | tf_op jit(solution)/shard_map/ppermute | solution.py:18
  91.7 5.5 copy-start.5
  91.7 205.2 %copy-start.4 = (s32[128,8]{0,1:T(8,128)S(1)}, s32[128,8]{0,1:T(8,128)}, u32[]{:S(2)}) copy-start(s32[128,8]{0,1:T(8,128)} %param.8) | copy-start | bytes 12292
  94.6 234.6 %collective-permute-start.2 = (bf16[4,128,4096]{2,1,0:T(8,128)(2,1)}, bf16[4,128,4096]{2,1,0:T(8,128)(2,1)}, u32[]{:S(2)}, u32[]{:S(2)}) collective-permute-start(bf16[4,128,4096]{2,1,0:T(8,128)(2,1)} %bitcast.7), channel_id=1, source_target_pairs={{0,16},{4,20},{8,24},{12,28},{16,0},{20,4},{24,8},{28,12},{1,17},{... | collective-permute-start | bytes 12582920 | tf_op jit(solution)/shard_map/ppermute | solution.py:18
  350.2 8.4 %copy-start.1 = (bf16[2,4,128,4096]{3,2,1,0:T(8,128)(2,1)S(1)}, bf16[2,4,128,4096]{3,2,1,0:T(8,128)(2,1)}, u32[]{:S(2)}) copy-start(bf16[2,4,128,4096]{3,2,1,0:T(8,128)(2,1)} %reverse_select_fusion) | copy-start | bytes 25165828
  358.6 17.6 %copy-start.6 = (bf16[2,2048,384]{2,1,0:T(8,128)(2,1)S(1)}, bf16[2,2048,384]{2,1,0:T(8,128)(2,1)}, u32[]{:S(2)}) copy-start(bf16[2,2048,384]{2,1,0:T(8,128)(2,1)} %param.12) | copy-start | bytes 9437188
  376.2 2.9 copy-start.2
  388.1 2.9 copy-start.7
  388.1 2.9 copy-start.3
  388.2 2.9 copy-start.8
  404.9 167.7 %reduce-scatter.4.cloned.1.call-start = ((), (), s32[]{:S(2)}) async-start(), calls=%async_computation.3 | async-start | bytes 4718592 | tf_op jit(solution)/shard_map/reduce_scatter | solution.py:72
  416.7 248.0 %reduce-scatter.6.cloned.1.call-start = ((), (), s32[]{:S(2)}) async-start(), calls=%async_computation.4 | async-start | bytes 4718592 | tf_op jit(solution)/shard_map/reduce_scatter | solution.py:87
Sparse Core Ops, SparseCore 0:
  405.0 74.9 reduce-scatter.7
  484.2 88.2 reduce-scatter.3
  576.8 87.9 reduce-scatter.5
